TPU v7x, 32 devices: a whole 2x2x4 slice. The times are simulated.
32 devices in a mesh: seq: 8 (over z, core), chan: 4 (over y, x).
Axes of the slice: x: 2, y: 2, z: 4, core: 2. Of those that a mesh axis runs over, the one named last changes fastest.
Arguments:
- gate_raw: bfloat16 [8, 2048, 2048], P('seq', None, 'chan'), may hold values from -50 to 50
- value_raw: bfloat16 [8, 2048, 2048], P('seq', None, 'chan'), may hold values from -50 to 50
- filter_gate: float32 [7, 2048], P(None, 'chan'), may hold values from -3 to 3
- filter_value: float32 [7, 2048], P(None, 'chan'), may hold values from -3 to 3
- teacher: float32 [8, 2048, 2048], P('seq', 'chan'), may hold values from -0.25 to 1, as said below
Outputs:
- grad_gate_raw: bfloat16 [8, 2048, 2048], P('seq', None, 'chan')
- grad_value_raw: bfloat16 [8, 2048, 2048], P('seq', None, 'chan')
- grad_filter_gate: float32 [7, 2048], P(None, 'chan')
- grad_filter_value: float32 [7, 2048], P(None, 'chan')
Inputs may be any that keep to these rules, and one draw needn't show every extreme that they name: teacher[s] is symmetric for each of the 8 sequences, with ones on its diagonal.
All inputs are finite; a program needn't handle non-finite values.
Results may differ from a plain program's by a relative error of at most 0.0059.
Values may be sent and summed in bfloat16 or wider, within the bound.
A program may use at most 128 MiB of HBM per device.

v0:
```python
import math
import jax
import jax.numpy as jnp
from jax import lax
from jax.sharding import PartitionSpec as P

TAPS = 7
epsilon = 1e-06


def causal_conv(signal, weights):
    length = signal.shape[1]
    padded = jnp.pad(signal, ((0, 0), (TAPS - 1, 0), (0, 0)))
    summed = jnp.zeros(signal.shape, jnp.float32)
    for tap_index in range(TAPS):
        window = padded[:, TAPS - 1 - tap_index : TAPS - 1 - tap_index + length]
        summed = summed + weights[tap_index] * window.astype(jnp.float32)
    return summed


def adjoint_conv(upstream, weights):
    length = upstream.shape[1]
    padded = jnp.pad(upstream, ((0, 0), (0, TAPS - 1), (0, 0)))
    summed = jnp.zeros(upstream.shape, jnp.float32)
    for tap_index in range(TAPS):
        summed = summed + weights[tap_index] * padded[:, tap_index : tap_index + length]
    return summed


def tap_sums(upstream, signal):
    length = signal.shape[1]
    padded = jnp.pad(signal, ((0, 0), (TAPS - 1, 0), (0, 0)))
    return jnp.stack(
        [
            jnp.sum(
                upstream
                * padded[:, TAPS - 1 - tap_index : TAPS - 1 - tap_index + length].astype(
                    jnp.float32
                ),
                axis=(0, 1),
            )
            for tap_index in range(TAPS)
        ]
    )


def gram_rows(normed, offset, stripe, teacher, factor, full_width):
    own_rows = lax.dynamic_slice_in_dim(normed, offset, stripe, 1)
    similarity = (
        jnp.einsum("srd,std->srt", own_rows, normed, preferred_element_type=jnp.float32)
        / full_width
    )
    residue = (factor * (similarity - teacher)).astype(jnp.bfloat16)
    return jnp.einsum("srt,std->srd", residue, normed, preferred_element_type=jnp.float32)


def on_device(gate_raw, value_raw, filter_gate, filter_value, teacher):
    seq_count, length, local_width = gate_raw.shape
    groups = lax.axis_size("chan")
    stripe = length // groups
    offset = lax.axis_index("chan") * stripe
    full_width = local_width * groups
    factor = 16.0 / math.sqrt(length)
    gate_conv = causal_conv(gate_raw, filter_gate)
    value_conv = causal_conv(value_raw, filter_value)
    hidden = (gate_conv * value_conv).astype(jnp.bfloat16)
    hidden_f = hidden.astype(jnp.float32)
    square_total = lax.psum(jnp.sum(hidden_f * hidden_f, axis=2), "chan")
    inv_rms = lax.rsqrt(square_total[:, :, None] / full_width + epsilon)
    normed_f = hidden_f * inv_rms
    normed = lax.all_gather(normed_f.astype(jnp.bfloat16), "chan", axis=2, tiled=True)
    row_part = gram_rows(normed, offset, stripe, teacher, factor, full_width)
    normed_grad = lax.all_to_all(row_part, "chan", split_axis=2, concat_axis=1, tiled=True)
    projection = lax.psum(jnp.sum(normed_f * normed_grad, axis=2) / full_width, "chan")
    hidden_grad = inv_rms * (normed_grad - normed_f * projection[:, :, None])
    gate_conv_grad = hidden_grad * value_conv
    value_conv_grad = hidden_grad * gate_conv
    grad_gate = adjoint_conv(gate_conv_grad, filter_gate).astype(jnp.bfloat16)
    grad_value = adjoint_conv(value_conv_grad, filter_value).astype(jnp.bfloat16)
    norm_factor = 1.0 / math.sqrt(lax.axis_size("seq") * seq_count * length)
    gate_taps, value_taps = lax.psum(
        (tap_sums(gate_conv_grad, gate_raw), tap_sums(value_conv_grad, value_raw)), "seq"
    )
    return (grad_gate, grad_value, gate_taps * norm_factor, value_taps * norm_factor)


def solution(mesh):
    placed = (
        P("seq", None, "chan"),
        P("seq", None, "chan"),
        P(None, "chan"),
        P(None, "chan"),
        P("seq", "chan", None),
    )
    return jax.shard_map(
        on_device,
        mesh=mesh,
        in_specs=placed,
        out_specs=(
            P("seq", None, "chan"),
            P("seq", None, "chan"),
            P(None, "chan"),
            P(None, "chan"),
        ),
        check_vma=False,
    )
```

profile of v0, /device:TPU:0, one launch (start us, length us, event | category | flops | bytes accessed | tf_op | source)
XLA Modules:
  0.0 296.8 jit_solution(16219476741442778253)
XLA Ops:
  7.2 0.0 all-gather.2.cloned.1.call-start
  7.2 1.0 fusion.66
  8.2 1.0 fusion.65
  9.2 18.7 %fusion.36 = (f32[2048]{0:T(1024)S(1)}, bf16[1,2048,512]{2,1,0:T(8,128)(2,1)S(1)}, f32[1,2048,512]{2,1,0:T(8,128)}, f32[1,2048,512]{2,1,0:T(8,128)}) fusion(f32[512]{0:T(512)S(1)} %bitcast.91, f32[512]{0:T(512)S(1)} %bitcast.93, f32[512]{0:T(512)S(1)} %bitcast.83, f32[512]{0:T(512)S(1)} %bitcast.85, f32[512]{0:T(512)S(1)} %bitcast.87, ...), kind=kLoop, calls=%fused_computation.66 | loop fusion | flops 47183872 | bytes 14716928 | tf_op jit(solution)/shard_map/reduce_sum | solution.py:68
  27.9 11.5 %psum.28 = f32[1,2048]{1,0:T(1,128)S(1)} all-reduce(f32[1,2048]{1,0:T(1,128)S(1)} %bitcast.80), channel_id=1, replica_groups=mesh['seq'=8,'chan'=4] {'chan'}, use_global_device_ids=true, to_apply=%region_1.2 | all-reduce | flops 2048 | bytes 16384 | tf_op jit(solution)/shard_map/psum | solution.py:68
  39.5 1.8 fusion.6
  41.3 0.0 all-gather.2.cloned.1.call-update
  41.3 86.9 %all-gather.2.cloned.1.call-done = bf16[1,2048,2048]{2,1,0:T(8,128)(2,1)} async-done(((bf16[1,2048,512]{2,1,0:T(8,128)(2,1)}), bf16[1,2048,2048]{2,1,0:T(8,128)(2,1)}) %all-gather.2.cloned.1.call-update) | async-done | bytes 8388624 | tf_op jit(solution)/shard_map/all_gather | solution.py:71
  128.1 18.4 %fusion.41 = f32[1,512,2048]{2,1,0:T(8,128)} fusion(bf16[1,2048,2048]{2,1,0:T(8,128)(2,1)} %all-gather.2.cloned.1.call-done, f32[1,512,2048]{2,1,0:T(8,128)} %param.9, s32[]{:T(128)S(6)} %select_n.3), kind=kOutput, calls=%fused_computation.73 | convolution fusion | flops 8594128896 | bytes 27262980 | tf_op jit(solution)/shard_map/srt,std->srd/dot_general | solution.py:54
  146.5 10.9 %copy.10 = f32[1,512,2048]{1,0,2:T(1,128)} copy(f32[1,512,2048]{2,1,0:T(8,128)} %fusion.41) | data formatting | bytes 8388608 | tf_op jit(solution)/shard_map/srt,std->srd/dot_general | solution.py:54
  157.4 53.7 %all_to_all.18 = f32[1,512,2048]{1,0,2:T(1,128)} all-to-all(f32[1,512,2048]{1,0,2:T(1,128)} %copy.10), channel_id=1, replica_groups=mesh['seq'=8,'chan'=4] {'chan'}, dimensions={2} | all-to-all | bytes 8388608 | tf_op jit(solution)/shard_map/all_to_all | solution.py:73
  211.1 10.9 %copy.11 = f32[1,4,512,512]{3,2,1,0:T(8,128)} copy(f32[1,4,512,512]{2,0,3,1:T(1,128)} %bitcast.75) | data formatting | bytes 8388608 | tf_op jit(solution)/shard_map/all_to_all | solution.py:73
  222.0 3.2 %fusion.33 = f32[2048]{0:T(1024)S(1)} fusion(bf16[1,2048,512]{2,1,0:T(8,128)(2,1)S(1)} %get-tuple-element.23, f32[1,4,512,512]{3,2,1,0:T(8,128)} %copy.11, f32[2048]{0:T(1024)S(1)} %bitcast.77), kind=kLoop, calls=%fused_computation.63 | loop fusion | flops 4192256 | bytes 6307840 | tf_op jit(solution)/shard_map/reduce_sum | solution.py:74
  225.2 8.7 %psum.29 = f32[2048]{0:T(1024)S(1)} all-reduce(f32[2048]{0:T(1024)S(1)} %broadcast_multiply_fusion.2), channel_id=1, replica_groups=mesh['seq'=8,'chan'=4] {'chan'}, use_global_device_ids=true, to_apply=%region_3.4 | all-reduce | flops 2048 | bytes 16384 | tf_op jit(solution)/shard_map/psum | solution.py:74
  233.9 0.0 copy-start
  233.9 0.0 copy-start.1
  234.0 0.0 copy-start.2
  234.0 15.5 %fusion.32 = (f32[512]{0:T(512)S(1)}, f32[512]{0:T(512)S(1)}, f32[512]{0:T(512)S(1)}, f32[512]{0:T(512)S(1)}, f32[512]{0:T(512)S(1)}, /*index=5*/f32[512]{0:T(512)S(1)}, f32[512]{0:T(512)S(1)}, f32[1,2048,512]{2,1,0:T(8,128)S(1)}) fusion(bf16[1,2048,512]{2,1,0:T(8,128)(2,1)} %param.6, f32[1,2048,512]{2,1,0:T(8,128)} %get-tuple-element.24, ...), kind=kLoop, calls=%fused_computation.62 | loop fusion | flops 28307968 | bytes 16807936 | tf_op jit(solution)/shard_map/reduce_sum | solution.py:35
  249.5 0.0 copy-done
  249.5 0.0 copy-done.1
  249.5 5.7 %fusion.19 = (f32[512]{0:T(512)S(1)}, f32[512]{0:T(512)S(1)}, f32[512]{0:T(512)S(1)}, f32[512]{0:T(512)S(1)}, f32[512]{0:T(512)S(1)}, /*index=5*/f32[512]{0:T(512)S(1)}, f32[512]{0:T(512)S(1)}, f32[1,2048,512]{2,1,0:T(8,128)S(1)}) fusion(bf16[1,2048,512]{2,1,0:T(8,128)(2,1)S(1)} %copy-done.2, f32[1,2048,512]{2,1,0:T(8,128)S(1)} %copy-done.1, ...), kind=kLoop, calls=%fused_computation.49 | loop fusion | flops 28307968 | bytes 16807936 | tf_op jit(solution)/shard_map/reduce_sum | solution.py:35
  255.2 8.1 %add_convert_fusion = (bf16[1,2048,512]{2,1,0:T(8,128)(2,1)}, bf16[1,2048,512]{2,1,0:T(8,128)(2,1)}) fusion(f32[1,2048,512]{2,1,0:T(8,128)S(1)} %get-tuple-element.20, f32[512]{0:T(512)S(1)} %bitcast.106, f32[512]{0:T(512)S(1)} %bitcast.108, f32[512]{0:T(512)S(1)} %bitcast.98, f32[512]{0:T(512)S(1)} %bitcast.100, f32[512]{0:T(512)S(1)} %bitcast.102, ...), kind=kLoop, calls=%fused_computation.70 | loop fusion | flops 29360128 | bytes 12611584 | tf_op jit(solution)/shard_map/convert_element_type | solution.py:79
  263.4 26.0 %all-reduce.4 = (f32[7,512]{1,0:T(8,128)S(1)}, f32[7,512]{1,0:T(8,128)S(1)}) all-reduce(f32[7,512]{1,0:T(8,128)S(1)} %stack.55, f32[7,512]{1,0:T(8,128)S(1)} %stack.63), channel_id=1, replica_groups=mesh['seq'=8,'chan'=4] {'seq'}, use_global_device_ids=true, to_apply=%region_11.12 | all-reduce | flops 7168 | bytes 57344 | tf_op jit(solution)/shard_map/psum | solution.py:81
  289.4 0.6 broadcast_multiply_fusion
  (5 shorter events, 0.1 us)
Async XLA Ops:
  7.2 121.0 %all-gather.2.cloned.1.call-start = ((), (), s32[]{:S(2)}) async-start(), calls=%async_computation.1 | async-start | bytes 10485760 | tf_op jit(solution)/shard_map/all_gather | solution.py:71
  233.9 15.5 %copy-start = (f32[1,4,512,512]{3,2,1,0:T(8,128)S(1)}, f32[1,4,512,512]{3,2,1,0:T(8,128)}, u32[]{:S(2)}) copy-start(f32[1,4,512,512]{3,2,1,0:T(8,128)} %copy.11) | copy-start | bytes 12582916
  233.9 15.5 %copy-start.1 = (f32[1,2048,512]{2,1,0:T(8,128)S(1)}, f32[1,2048,512]{2,1,0:T(8,128)}, u32[]{:S(2)}) copy-start(f32[1,2048,512]{2,1,0:T(8,128)} %get-tuple-element.25) | copy-start | bytes 12582916
  234.0 15.5 %copy-start.2 = (bf16[1,2048,512]{2,1,0:T(8,128)(2,1)S(1)}, bf16[1,2048,512]{2,1,0:T(8,128)(2,1)}, u32[]{:S(2)}) copy-start(bf16[1,2048,512]{2,1,0:T(8,128)(2,1)} %param.5) | copy-start | bytes 6291460
Sparse Core Ops, SparseCore 0:
  41.4 86.7 all-gather.1
where the time goes:
time: 298 us; the launch traced here: 297 us
  blocking collectives  99.9 us (34%)
  waiting for transfers between devices  86.9 us (29%)
  other arithmetic  53.6 us (18%)
  local copies, waits for them, and re-layouts  23.9 us (8%)
  matrix products  18.4 us (6%)
  between operations  14.1 us (5%)
    all_gather x1, waiting for transfers between devices, on_device(): lax.all_gather(normed_f.astype(jnp.bfloat16), 'chan', axis=2, tiled=True)  86.9 us
    all_to_all x1, blocking collectives, on_device(): lax.all_to_all(row_part, 'chan', split_axis=2, concat_axis=1, tiled=True)  53.7 us
    psum x1, blocking collectives, on_device(): lax.psum((tap_sums(gate_conv_grad, gate_raw), tap_sums(value_conv_grad, v...  26 us
    reduce_sum x2, other arithmetic, tap_sums(): jnp.sum(upstream * padded[:, TAPS - 1 - tap_index:TAPS - 1 - tap_index +...  21.2 us
    reduce_sum x1, other arithmetic, on_device(): square_total = lax.psum(jnp.sum(hidden_f * hidden_f, axis=2), 'chan')  18.7 us
    dot_general x1, matrix products, gram_rows(): jnp.einsum('srt,std->srd', residue, normed, preferred_element_type=jnp.fl...  18.4 us
    psum x1, blocking collectives, on_device(): square_total = lax.psum(jnp.sum(hidden_f * hidden_f, axis=2), 'chan')  11.5 us
    all_to_all x1, local copies, waits for them, and re-layouts, on_device(): lax.all_to_all(row_part, 'chan', split_axis=2, concat_axis=1, tiled=True)  10.9 us
  transfers between devices with their start and end apart: 1, of which 1 were waited for; matrix products, arithmetic and copies ran while one was open for 0% of the time, Pallas kernels for 0%

commit v1 on v0

--- a/solution.py
+++ b/solution.py
@@ -70,7 +70,10 @@
     normed_f = hidden_f * inv_rms
     normed = lax.all_gather(normed_f.astype(jnp.bfloat16), "chan", axis=2, tiled=True)
     row_part = gram_rows(normed, offset, stripe, teacher, factor, full_width)
-    normed_grad = lax.all_to_all(row_part, "chan", split_axis=2, concat_axis=1, tiled=True)
+    normed_grad = jnp.concatenate(
+        lax.all_to_all(jnp.stack(jnp.split(row_part, lax.axis_size("chan"), axis=2)), "chan", 0, 0),
+        axis=1,
+    )
     projection = lax.psum(jnp.sum(normed_f * normed_grad, axis=2) / full_width, "chan")
     hidden_grad = inv_rms * (normed_grad - normed_f * projection[:, :, None])
     gate_conv_grad = hidden_grad * value_conv

time: 298 us -> 275 us (0.923)
  local copies, waits for them, and re-layouts: 23.9 us -> 6.61 us
  blocking collectives: 99.9 us -> 96.8 us
    all_to_all x1 -> x0, local copies, waits for them, and re-layouts: 10.9 us -> none  [on_device(): lax.all_to_all(row_part, 'chan', split_axis=2, concat_axis=1, tiled=True)]
    dot_general x1 -> x0, local copies, waits for them, and re-layouts: 10.9 us -> none  [gram_rows(): jnp.einsum('srt,std->srd', residue, normed, preferred_element_type=jnp.fl...]
    all_to_all x1, blocking collectives: 53.7 us -> 50.5 us  [on_device(): lax.all_to_all(jnp.stack(jnp.split(row_part, lax.axis_size('chan'), axis=...]
where the time goes in v1:
time: 275 us; the launch traced here: 274 us
  blocking collectives  96.8 us (35%)
  waiting for transfers between devices  86.9 us (32%)
  other arithmetic  51.5 us (19%)
  matrix products  18.4 us (7%)
  between operations  14.2 us (5%)
  local copies, waits for them, and re-layouts  6.61 us (2%)
    all_gather x1, waiting for transfers between devices, on_device(): lax.all_gather(normed_f.astype(jnp.bfloat16), 'chan', axis=2, tiled=True)  86.9 us
    all_to_all x1, blocking collectives, on_device(): lax.all_to_all(jnp.stack(jnp.split(row_part, lax.axis_size('chan'), axis=...  50.5 us
    psum x1, blocking collectives, on_device(): lax.psum((tap_sums(gate_conv_grad, gate_raw), tap_sums(value_conv_grad, v...  26 us
    reduce_sum x2, other arithmetic, tap_sums(): jnp.sum(upstream * padded[:, TAPS - 1 - tap_index:TAPS - 1 - tap_index +...  20.8 us
    reduce_sum x1, other arithmetic, on_device(): square_total = lax.psum(jnp.sum(hidden_f * hidden_f, axis=2), 'chan')  18.7 us
    dot_general x1, matrix products, gram_rows(): jnp.einsum('srt,std->srd', residue, normed, preferred_element_type=jnp.fl...  18.4 us
    psum x1, blocking collectives, on_device(): square_total = lax.psum(jnp.sum(hidden_f * hidden_f, axis=2), 'chan')  11.5 us
    psum x1, blocking collectives, on_device(): lax.psum(jnp.sum(normed_f * normed_grad, axis=2) / full_width, 'chan')  8.74 us
  transfers between devices with their start and end apart: 1, of which 1 were waited for; matrix products, arithmetic and copies ran while one was open for 0% of the time, Pallas kernels for 0%

profile of v1, /device:TPU:0, one launch (start us, length us, event | category | flops | bytes accessed | tf_op | source)
XLA Modules:
  0.0 274.4 jit_solution(15678963234167951332)
XLA Ops:
  7.2 0.0 all-gather.2.cloned.1.call-start
  7.2 1.0 fusion.66
  8.2 1.0 fusion.65
  9.2 18.7 %fusion.36 = (f32[2048]{0:T(1024)S(1)}, bf16[1,2048,512]{2,1,0:T(8,128)(2,1)S(1)}, f32[1,2048,512]{2,1,0:T(8,128)}, f32[1,2048,512]{2,1,0:T(8,128)}) fusion(f32[512]{0:T(512)S(1)} %bitcast.90, f32[512]{0:T(512)S(1)} %bitcast.92, f32[512]{0:T(512)S(1)} %bitcast.82, f32[512]{0:T(512)S(1)} %bitcast.84, f32[512]{0:T(512)S(1)} %bitcast.86, ...), kind=kLoop, calls=%fused_computation.66 | loop fusion | flops 47183872 | bytes 14716928 | tf_op jit(solution)/shard_map/reduce_sum | solution.py:68
  27.9 11.5 %psum.28 = f32[1,2048]{1,0:T(1,128)S(1)} all-reduce(f32[1,2048]{1,0:T(1,128)S(1)} %bitcast.79), channel_id=1, replica_groups=mesh['seq'=8,'chan'=4] {'chan'}, use_global_device_ids=true, to_apply=%region_1.2 | all-reduce | flops 2048 | bytes 16384 | tf_op jit(solution)/shard_map/psum | solution.py:68
  39.5 1.8 fusion.6
  41.3 0.0 all-gather.2.cloned.1.call-update
  41.3 86.9 %all-gather.2.cloned.1.call-done = bf16[1,2048,2048]{2,1,0:T(8,128)(2,1)} async-done(((bf16[1,2048,512]{2,1,0:T(8,128)(2,1)}), bf16[1,2048,2048]{2,1,0:T(8,128)(2,1)}) %all-gather.2.cloned.1.call-update) | async-done | bytes 8388624 | tf_op jit(solution)/shard_map/all_gather | solution.py:71
  128.1 18.4 %fusion.41 = f32[1,512,2048]{2,1,0:T(8,128)} fusion(bf16[1,2048,2048]{2,1,0:T(8,128)(2,1)} %all-gather.2.cloned.1.call-done, f32[1,512,2048]{2,1,0:T(8,128)} %param.9, s32[]{:T(128)S(6)} %select_n.3), kind=kOutput, calls=%fused_computation.74 | convolution fusion | flops 8594128896 | bytes 27262980 | tf_op jit(solution)/shard_map/srt,std->srd/dot_general | solution.py:54
  146.5 2.6 slice_bitcast_fusion.3
  149.2 0.4 pad_maximum_fusion
  149.6 50.5 %all_to_all.5 = f32[4,1,512,512]{3,2,1,0:T(8,128)S(1)} all-to-all(f32[4,1,512,512]{3,2,1,0:T(8,128)S(1)} %pad_maximum_fusion), channel_id=1, replica_groups=mesh['seq'=8,'chan'=4] {'chan'}, dimensions={0} | all-to-all | bytes 8388608 | tf_op jit(solution)/shard_map/all_to_all | solution.py:74
  200.1 1.9 copy-done
  202.1 1.0 fusion.33
  203.1 8.7 %psum.29 = f32[2048]{0:T(1024)S(1)} all-reduce(f32[2048]{0:T(1024)S(1)} %broadcast_multiply_fusion.2), channel_id=1, replica_groups=mesh['seq'=8,'chan'=4] {'chan'}, use_global_device_ids=true, to_apply=%region_3.4 | all-reduce | flops 2048 | bytes 16384 | tf_op jit(solution)/shard_map/psum | solution.py:77
  211.8 0.0 copy-start.1
  211.8 0.0 copy-start.2
  211.8 0.0 copy-start.3
  211.9 15.5 %fusion.32 = (f32[512]{0:T(512)S(1)}, f32[512]{0:T(512)S(1)}, f32[512]{0:T(512)S(1)}, f32[512]{0:T(512)S(1)}, f32[512]{0:T(512)S(1)}, /*index=5*/f32[512]{0:T(512)S(1)}, f32[512]{0:T(512)S(1)}, f32[1,2048,512]{2,1,0:T(8,128)S(1)}) fusion(bf16[1,2048,512]{2,1,0:T(8,128)(2,1)} %param.6, f32[1,2048,512]{2,1,0:T(8,128)} %get-tuple-element.24, ...), kind=kLoop, calls=%fused_computation.62 | loop fusion | flops 28307968 | bytes 16807936 | tf_op jit(solution)/shard_map/reduce_sum | solution.py:35
  227.4 0.0 copy-done.1
  227.4 5.3 %fusion.19 = (f32[512]{0:T(512)S(1)}, f32[512]{0:T(512)S(1)}, f32[512]{0:T(512)S(1)}, f32[512]{0:T(512)S(1)}, f32[512]{0:T(512)S(1)}, /*index=5*/f32[512]{0:T(512)S(1)}, f32[512]{0:T(512)S(1)}, f32[1,2048,512]{2,1,0:T(8,128)S(1)}) fusion(bf16[1,2048,512]{2,1,0:T(8,128)(2,1)S(1)} %copy-done.3, f32[1,2048,512]{2,1,0:T(8,128)S(1)} %copy-done.2, ...), kind=kLoop, calls=%fused_computation.49 | loop fusion | flops 28307968 | bytes 16807936 | tf_op jit(solution)/shard_map/reduce_sum | solution.py:35
  232.7 8.1 %add_convert_fusion = (bf16[1,2048,512]{2,1,0:T(8,128)(2,1)}, bf16[1,2048,512]{2,1,0:T(8,128)(2,1)}) fusion(f32[1,2048,512]{2,1,0:T(8,128)S(1)} %get-tuple-element.20, f32[512]{0:T(512)S(1)} %bitcast.105, f32[512]{0:T(512)S(1)} %bitcast.107, f32[512]{0:T(512)S(1)} %bitcast.97, f32[512]{0:T(512)S(1)} %bitcast.99, f32[512]{0:T(512)S(1)} %bitcast.101, ...), kind=kLoop, calls=%fused_computation.71 | loop fusion | flops 29360128 | bytes 12611584 | tf_op jit(solution)/shard_map/convert_element_type | solution.py:82
  240.9 26.0 %all-reduce.4 = (f32[7,512]{1,0:T(8,128)S(1)}, f32[7,512]{1,0:T(8,128)S(1)}) all-reduce(f32[7,512]{1,0:T(8,128)S(1)} %stack.75, f32[7,512]{1,0:T(8,128)S(1)} %stack.83), channel_id=1, replica_groups=mesh['seq'=8,'chan'=4] {'seq'}, use_global_device_ids=true, to_apply=%region_11.12 | all-reduce | flops 7168 | bytes 57344 | tf_op jit(solution)/shard_map/psum | solution.py:84
  266.9 0.6 broadcast_multiply_fusion
  (7 shorter events, 0.1 us)
Async XLA Ops:
  7.2 121.0 %all-gather.2.cloned.1.call-start = ((), (), s32[]{:S(2)}) async-start(), calls=%async_computation.1 | async-start | bytes 10485760 | tf_op jit(solution)/shard_map/all_gather | solution.py:71
  200.1 1.9 copy-start
  211.8 15.5 %copy-start.1 = (f32[4,1,512,512]{3,2,1,0:T(8,128)S(1)}, f32[4,1,512,512]{3,2,1,0:T(8,128)}, u32[]{:S(2)}) copy-start(f32[4,1,512,512]{3,2,1,0:T(8,128)} %copy-done) | copy-start | bytes 12582916
  211.8 15.5 %copy-start.2 = (f32[1,2048,512]{2,1,0:T(8,128)S(1)}, f32[1,2048,512]{2,1,0:T(8,128)}, u32[]{:S(2)}) copy-start(f32[1,2048,512]{2,1,0:T(8,128)} %get-tuple-element.25) | copy-start | bytes 12582916
  211.8 15.5 %copy-start.3 = (bf16[1,2048,512]{2,1,0:T(8,128)(2,1)S(1)}, bf16[1,2048,512]{2,1,0:T(8,128)(2,1)}, u32[]{:S(2)}) copy-start(bf16[1,2048,512]{2,1,0:T(8,128)(2,1)} %param.5) | copy-start | bytes 6291460
Sparse Core Ops, SparseCore 0:
  41.4 86.7 all-gather.1
